TPU v7x, 32 devices: a whole 2x2x4 slice. The times are simulated.
32 devices in a mesh: groups: 1, ep: 16 (over z, y, x), tp: 2 (over core).
Axes of the slice: x: 2, y: 2, z: 4, core: 2. Of those that a mesh axis runs over, the one named last changes fastest.
Arguments:
- tokens: bfloat16 [1024, 4096], P(('groups', 'ep'), 'tp'), may hold values from -6 to 6
- w_down: bfloat16 [4096, 1024], P('tp', 'ep'), may hold values from -0.09375 to 0.09375
- w_in: bfloat16 [16, 1024, 1344], P('ep', None, 'tp'), may hold values from -0.1875 to 0.1875
- w_out: bfloat16 [16, 1344, 1024], P('ep', 'tp'), may hold values from -0.125 to 0.125
- w_up: bfloat16 [1024, 4096], P('ep', 'tp'), may hold values from -0.1875 to 0.1875
- expert_ids: int32 [1024, 3], P(('groups', 'ep')), may hold values from 0 to 7, all different within a row; in each aligned block of 64 rows (0 to 63, 64 to 127, ...) at most 48 rows name the same one
- route_weights: float32 [1024, 3], P(('groups', 'ep')), may hold values from 0.2 to 1
Outputs:
- layer_out: bfloat16 [1024, 4096], P(('groups', 'ep'), 'tp')
Inputs may be any that keep to these rules, and one draw needn't show every extreme that they name: `expert_ids`: each row names 3 different experts. In each aligned block of 64 rows (the rows of one device) no expert is named more than 48 times, a bound that some block reaches.
All inputs are finite; a program needn't handle non-finite values.
Results may differ from a plain program's by a relative error of at most 0.009.
Values may be sent and summed in bfloat16 or wider, within the bound.
A program may use at most 64 MiB of HBM per device.

v0:
```python
import jax
import jax.numpy as jnp
from jax import lax
from jax.sharding import PartitionSpec as P


def swapped(value, axis, apart):
    mask = 2**apart
    pairs = [(source, source ^ mask) for source in range(lax.axis_size(axis))]
    return lax.ppermute(value, axis, pairs)


def slot_tables(expert_ids, experts, capacity):
    count, top = expert_ids.shape
    flat = expert_ids.reshape(count * top)
    onehot = (flat[:, None] == jnp.arange(experts, dtype=jnp.int32)[None, :]).astype(jnp.int32)
    before = jnp.cumsum(onehot, axis=0) - onehot
    position = jnp.sum(before * onehot, axis=1)
    place = flat * capacity + position
    sender = jnp.arange(count * top, dtype=jnp.int32) // top
    owner = jnp.full((experts * capacity,), count, jnp.int32).at[place].set(sender)
    return (place, owner)


def per_device(tokens, w_down, w_in, w_out, w_up, expert_ids, route_weights):
    count, top = expert_ids.shape
    devices = lax.axis_size("ep")
    experts = devices // 2
    capacity = 2 * min(count // 2, max(1, count * top // experts))
    halfcap = capacity // 2
    partial_value = jnp.dot(
        tokens, lax.all_gather(w_down, "ep", axis=1, tiled=True), preferred_element_type=jnp.float32
    )
    place, owner = slot_tables(expert_ids, experts, capacity)
    live = owner < count
    source_row = jnp.minimum(owner, count - 1)
    latent = lax.psum(partial_value, "tp").astype(jnp.bfloat16)
    outgoing = latent[source_row]
    outgoing = jnp.where(live[:, None], outgoing, jnp.zeros_like(outgoing))
    outgoing = outgoing.reshape(experts, capacity, outgoing.shape[1])
    outgoing = outgoing.reshape(devices, halfcap, outgoing.shape[2])
    arrived = lax.all_to_all(outgoing, "ep", split_axis=0, concat_axis=0, tiled=True)
    parity = lax.axis_index("ep") % 2
    partner = swapped(arrived, "ep", 0)
    arrived = jnp.where(
        parity == 0,
        jnp.concatenate([arrived, partner], axis=1),
        jnp.concatenate([partner, arrived], axis=1),
    )
    rows = arrived.reshape(devices * capacity, arrived.shape[2])
    pre = jnp.maximum(jnp.dot(rows, w_in[0], preferred_element_type=jnp.float32), 0.0)
    hidden = (pre * pre).astype(jnp.bfloat16)
    result = jnp.dot(hidden, w_out[0], preferred_element_type=jnp.float32)
    result = result.reshape(devices, capacity, result.shape[1])
    width = result.shape[2]
    feature_half = width // 2
    lower = result[:, :, :feature_half]
    upper = result[:, :, feature_half:]
    mine = jnp.where(parity == 0, lower, upper)
    theirs = jnp.where(parity == 0, upper, lower)
    sending = mine + swapped(theirs.astype(jnp.bfloat16), "ep", 0).astype(theirs.dtype)
    returned = lax.all_to_all(sending, "ep", split_axis=0, concat_axis=0, tiled=True)
    summed = returned.reshape(experts, 2, capacity, width // 2)
    summed = jnp.transpose(summed, (0, 2, 1, 3)).reshape(experts * capacity, width)
    picked = summed[place] * route_weights.reshape(count * top)[:, None]
    mixed_part = jnp.sum(picked.reshape(count, top, width), axis=1)
    mixed = lax.psum(mixed_part, "tp").astype(jnp.bfloat16)
    layer_out = jnp.dot(
        mixed, lax.all_gather(w_up, "ep", axis=0, tiled=True), preferred_element_type=jnp.float32
    )
    return layer_out.astype(jnp.bfloat16)


def solution(mesh):
    in_specs = (
        P(("groups", "ep"), "tp"),
        P("tp", "ep"),
        P("ep", None, "tp"),
        P("ep", "tp", None),
        P("ep", "tp"),
        P(("groups", "ep"), None),
        P(("groups", "ep"), None),
    )
    out_specs = P(("groups", "ep"), "tp")
    return jax.shard_map(
        per_device, mesh=mesh, in_specs=in_specs, out_specs=out_specs, check_vma=False
    )
```

profile of v0, /device:TPU:0, one launch (start us, length us, event | category | flops | bytes accessed | tf_op | source)
XLA Modules:
  0.0 244.3 jit_solution(5072719154304027839)
XLA Ops:
  6.5 0.7 all-gather.3.cloned.1.call-update
  7.3 0.8 copy.12
  8.2 0.6 reduce-window.6
  8.8 0.2 slice_reduce_fusion
  9.0 0.7 broadcast_multiply_fusion
  10.1 1.2 scatter_custom_fusion
  11.4 77.0 %all-gather.3.cloned.1.call-done = bf16[2048,1024]{0,1:T(8,128)(2,1)} async-done(((bf16[2048,64]{0,1:T(8,128)(2,1)}), bf16[2048,1024]{0,1:T(8,128)(2,1)}) %all-gather.3.cloned.1.call-update) | async-done | bytes 4194320 | tf_op jit(solution)/shard_map/all_gather | solution.py:32
  88.4 3.7 %fusion.8 = f32[64,1024]{1,0:T(8,128)S(1)} fusion(bf16[64,2048]{1,0:T(8,128)(2,1)} %param.7, bf16[2048,1024]{0,1:T(8,128)(2,1)} %all-gather.3.cloned.1.call-done), kind=kOutput, calls=%fused_computation.34 | convolution fusion | flops 268435456 | bytes 4718592 | tf_op jit(solution)/shard_map/dot_general | solution.py:31
  92.1 4.2 %all-reduce.3 = bf16[64,1024]{1,0:T(8,128)(2,1)S(1)} all-reduce(f32[64,1024]{1,0:T(8,128)S(1)} %fusion.8), channel_id=1, replica_groups=mesh['groups'=1,'ep'=16,'tp'=2] {'tp'}, use_global_device_ids=true, to_apply=%region_4.5 | all-reduce | flops 65536 | bytes 393216 | tf_op jit(solution)/shard_map/psum | solution.py:37
  96.3 2.1 gather_fusion
  98.4 1.0 broadcast_select_fusion
  99.4 4.2 %all-to-all-start = ((bf16[16,24,1024]{2,1,0:T(8,128)(2,1)}), bf16[16,24,1024]{2,1,0:T(8,128)(2,1)S(1)}, u32[]{:S(2)}, u32[]{:S(2)}) async-start(bf16[16,24,1024]{2,1,0:T(8,128)(2,1)} %broadcast_select_fusion), calls=%async_computation | async-start | bytes 1572864 | tf_op jit(solution)/shard_map/all_to_all | solution.py:42
  103.7 0.7 all-gather.5.cloned.1.call-update
  104.4 21.3 %all-to-all-done = bf16[16,24,1024]{2,1,0:T(8,128)(2,1)S(1)} async-done(((bf16[16,24,1024]{2,1,0:T(8,128)(2,1)}), bf16[16,24,1024]{2,1,0:T(8,128)(2,1)S(1)}, u32[]{:S(2)}, u32[]{:S(2)}) %all-to-all-start) | async-done | bytes 786464 | tf_op jit(solution)/shard_map/all_to_all | solution.py:42
  125.7 0.4 collective-permute-start
  126.1 22.4 %collective-permute-done = bf16[16,24,1024]{2,1,0:T(8,128)(2,1)S(1)} collective-permute-done((bf16[16,24,1024]{2,1,0:T(8,128)(2,1)S(1)}, bf16[16,24,1024]{2,1,0:T(8,128)(2,1)S(1)}, u32[]{:S(2)}, u32[]{:S(2)}) %collective-permute-start) | collective-permute-done | bytes 786464 | tf_op jit(solution)/shard_map/ppermute | solution.py:10
  148.6 0.7 maximum_select_fusion
  149.3 2.3 multiply_convert_fusion
  151.5 1.5 copy.13
  153.1 1.4 fusion
  154.6 2.5 %collective-permute-start.1 = (bf16[16,48,512]{2,1,0:T(8,128)(2,1)S(1)}, bf16[16,48,512]{2,1,0:T(8,128)(2,1)S(1)}, u32[]{:S(2)}, u32[]{:S(2)}) collective-permute-start(bf16[16,48,512]{2,1,0:T(8,128)(2,1)S(1)} %select_convert_fusion), channel_id=1, source_target_pairs={{0,2},{2,0},{4,6},{6,4},{8,10},{10,8},{12,14},{14,12},{16,18},{18,... | collective-permute-start | bytes 2359304 | tf_op jit(solution)/shard_map/ppermute | solution.py:10
  157.2 18.7 %collective-permute-done.1 = bf16[16,48,512]{2,1,0:T(8,128)(2,1)S(1)} collective-permute-done((bf16[16,48,512]{2,1,0:T(8,128)(2,1)S(1)}, bf16[16,48,512]{2,1,0:T(8,128)(2,1)S(1)}, u32[]{:S(2)}, u32[]{:S(2)}) %collective-permute-start.1) | collective-permute-done | bytes 786464 | tf_op jit(solution)/shard_map/ppermute | solution.py:10
  175.9 1.6 convert_add_fusion
  177.5 23.0 %all-to-all-start.1 = ((f32[16,48,512]{2,1,0:T(8,128)}), f32[16,48,512]{2,1,0:T(8,128)S(1)}, u32[]{:S(2)}, u32[]{:S(2)}) async-start(f32[16,48,512]{2,1,0:T(8,128)} %convert_add_fusion), calls=%async_computation.1 | async-start | bytes 3145728 | tf_op jit(solution)/shard_map/all_to_all | solution.py:62
  200.6 23.4 %all-to-all-done.1 = f32[16,48,512]{2,1,0:T(8,128)S(1)} async-done(((f32[16,48,512]{2,1,0:T(8,128)}), f32[16,48,512]{2,1,0:T(8,128)S(1)}, u32[]{:S(2)}, u32[]{:S(2)}) %all-to-all-start.1) | async-done | bytes 1572896 | tf_op jit(solution)/shard_map/all_to_all | solution.py:62
  224.0 1.2 copy.14
  225.2 0.3 copy.16
  225.5 1.8 gather_fusion.1
  227.3 1.5 gather.13
  228.8 0.7 multiply_reduce_fusion
  229.5 4.2 %all-reduce.4 = bf16[64,1024]{1,0:T(8,128)(2,1)S(1)} all-reduce(f32[64,1024]{1,0:T(8,128)S(1)} %multiply_reduce_fusion), channel_id=1, replica_groups=mesh['groups'=1,'ep'=16,'tp'=2] {'tp'}, use_global_device_ids=true, to_apply=%region_6.7 | all-reduce | flops 65536 | bytes 393216 | tf_op jit(solution)/shard_map/psum | solution.py:67
  233.7 3.7 %convolution_convert_fusion = bf16[64,2048]{1,0:T(8,128)(2,1)} fusion(bf16[1024,2048]{1,0:T(8,128)(2,1)} %all-gather.5.cloned.1.call-done, bf16[64,1024]{1,0:T(8,128)(2,1)S(1)} %all-reduce.4), kind=kOutput, calls=%fused_computation.3 | convolution fusion | flops 268566528 | bytes 4587520 | tf_op jit(solution)/shard_map/dot_general | solution.py:68
  (27 shorter events, 1.0 us)
Async XLA Ops:
  6.5 146.5 %copy-start = (bf16[1,672,1024]{2,1,0:T(8,128)(2,1)S(1)}, bf16[1,672,1024]{2,1,0:T(8,128)(2,1)}, u32[]{:S(2)}) copy-start(bf16[1,672,1024]{2,1,0:T(8,128)(2,1)} %param.10) | copy-start | bytes 4128772
  6.5 81.9 %all-gather.3.cloned.1.call-start = ((), (), s32[]{:S(2)}) async-start(), calls=%async_computation.2 | async-start | bytes 4456448 | tf_op jit(solution)/shard_map/all_gather | solution.py:32
  99.4 26.3 %all-to-all-start = ((bf16[16,24,1024]{2,1,0:T(8,128)(2,1)}), bf16[16,24,1024]{2,1,0:T(8,128)(2,1)S(1)}, u32[]{:S(2)}, u32[]{:S(2)}) async-start(bf16[16,24,1024]{2,1,0:T(8,128)(2,1)} %broadcast_select_fusion), calls=%async_computation | async-start | bytes 1572864 | tf_op jit(solution)/shard_map/all_to_all | solution.py:42
  103.6 130.1 %all-gather.5.cloned.1.call-start = ((), (), s32[]{:S(2)}) async-start(), calls=%async_computation.3 | async-start | bytes 4456448 | tf_op jit(solution)/shard_map/all_gather | solution.py:69
  125.7 22.9 %collective-permute-start = (bf16[16,24,1024]{2,1,0:T(8,128)(2,1)S(1)}, bf16[16,24,1024]{2,1,0:T(8,128)(2,1)S(1)}, u32[]{:S(2)}, u32[]{:S(2)}) collective-permute-start(bf16[16,24,1024]{2,1,0:T(8,128)(2,1)S(1)} %all-to-all-done), channel_id=1, source_target_pairs={{0,2},{2,0},{4,6},{6,4},{8,10},{10,8},{12,14},{14,12},{16,18},{18,... | collective-permute-start | bytes 2359304 | tf_op jit(solution)/shard_map/ppermute | solution.py:10
  126.1 23.1 %copy-start.2 = (bf16[1,1024,672]{1,2,0:T(8,128)(2,1)S(1)}, bf16[1,1024,672]{1,2,0:T(8,128)(2,1)}, u32[]{:S(2)}) copy-start(bf16[1,1024,672]{1,2,0:T(8,128)(2,1)} %param.9) | copy-start | bytes 4128772
  154.6 21.3 %collective-permute-start.1 = (bf16[16,48,512]{2,1,0:T(8,128)(2,1)S(1)}, bf16[16,48,512]{2,1,0:T(8,128)(2,1)S(1)}, u32[]{:S(2)}, u32[]{:S(2)}) collective-permute-start(bf16[16,48,512]{2,1,0:T(8,128)(2,1)S(1)} %select_convert_fusion), channel_id=1, source_target_pairs={{0,2},{2,0},{4,6},{6,4},{8,10},{10,8},{12,14},{14,12},{16,18},{18,... | collective-permute-start | bytes 2359304 | tf_op jit(solution)/shard_map/ppermute | solution.py:10
  177.5 23.0 %copy-start.1 = (f32[64,3]{0,1:T(4,128)S(1)}, f32[64,3]{0,1:T(4,128)}, u32[]{:S(2)}) copy-start(f32[64,3]{0,1:T(4,128)} %param.13) | copy-start | bytes 2308
  177.5 46.5 %all-to-all-start.1 = ((f32[16,48,512]{2,1,0:T(8,128)}), f32[16,48,512]{2,1,0:T(8,128)S(1)}, u32[]{:S(2)}, u32[]{:S(2)}) async-start(f32[16,48,512]{2,1,0:T(8,128)} %convert_add_fusion), calls=%async_computation.1 | async-start | bytes 3145728 | tf_op jit(solution)/shard_map/all_to_all | solution.py:62
Sparse Core Ops, SparseCore 0:
  10.1 78.3 all-gather.2
  107.2 98.6 all-gather.4
where the time goes:
time: 245 us; the launch traced here: 244 us
  waiting for transfers between devices  164 us (67%)
  starting transfers between devices  30.2 us (12%)
  between operations  13.6 us (6%)
  local copies, waits for them, and re-layouts  11.2 us (5%)
  matrix products  11.1 us (5%)
  blocking collectives  8.33 us (3%)
  other arithmetic  5.6 us (2%)
    all_gather x1, waiting for transfers between devices, per_device(): lax.all_gather(w_down, 'ep', axis=1, tiled=True)  77 us
    ppermute x2, waiting for transfers between devices, swapped(): return lax.ppermute(value, axis, pairs)  41.2 us
    all_to_all x1, waiting for transfers between devices, per_device(): lax.all_to_all(sending, 'ep', split_axis=0, concat_axis=0, tiled=True)  23.4 us
    all_to_all x1, starting transfers between devices, per_device(): lax.all_to_all(sending, 'ep', split_axis=0, concat_axis=0, tiled=True)  23 us
    all_to_all x1, waiting for transfers between devices, per_device(): lax.all_to_all(outgoing, 'ep', split_axis=0, concat_axis=0, tiled=True)  21.3 us
  transfers between devices with their start and end apart: 6, of which 5 were waited for; matrix products, arithmetic and copies ran while one was open for 7% of the time, Pallas kernels for 0%

commit v1 on v0

--- a/solution.py
+++ b/solution.py
@@ -1,7 +1,15 @@
+import functools
+
 import jax
 import jax.numpy as jnp
 from jax import lax
+from jax.experimental import pallas as pl
+from jax.experimental.pallas import tpu as pltpu
 from jax.sharding import PartitionSpec as P
+
+F32 = jnp.float32
+BF16 = jnp.bfloat16
+LANES = 128
 
 
 def swapped(value, axis, apart):
@@ -71,6 +79,217 @@
     return layer_out.astype(jnp.bfloat16)
 
 
+def fused_kernel(
+    lines, plane,
+    tok_ref, wd_ref, win_hbm, wout_hbm, wup_ref, ids_ref, rw_ref, out_ref,
+    tbuf, wbuf, gbuf, ubuf, part, other, latent, win, wout, ykeep, ysend, ycore,
+    xsend, yrecv, zsend, zrecv, mbuf, obuf, send_sem, recv_sem, local_sem,
+):
+    ep = lax.axis_index("ep")
+    core = lax.axis_index("tp")
+    p = lax.rem(ep, plane)
+    z = ep // plane
+    mate = 1 - core
+    rows, top = ids_ref.shape
+    group = lines * rows
+    half_rows = group // 2
+    cols = wd_ref.shape[0] * plane
+    feat = latent.shape[1] // 2
+    quarter = ubuf.shape[1]
+    ids = iter(range(send_sem.shape[0]))
+
+    def at_plane(j):
+        return {"ep": z * plane + (p ^ j), "tp": core}
+
+    def at_line(k):
+        return {"ep": (z ^ k) * plane + p, "tp": core}
+
+    at_mate = {"ep": ep, "tp": mate}
+    peers = [at_plane(j) for j in range(1, plane)] + [at_line(k) for k in range(1, lines)] + [at_mate]
+
+    def copy(src, dst, device):
+        i = next(ids)
+        return pltpu.make_async_remote_copy(
+            src_ref=src, dst_ref=dst, send_sem=send_sem.at[i], recv_sem=recv_sem.at[i],
+            device_id=device, device_id_type=pl.DeviceIdType.MESH,
+        )
+
+    started = []
+
+    def start(copies):
+        for c in copies:
+            c.start()
+            started.append(c)
+        return copies
+
+    def got(copies):
+        for c in copies:
+            c.wait_recv()
+
+    def block(index, size):
+        return pl.ds(pl.multiple_of(index * size, size), size)
+
+    load_in = pltpu.make_async_copy(win_hbm, win, local_sem.at[0])
+    load_out = pltpu.make_async_copy(wout_hbm, wout, local_sem.at[1])
+    load_in.start()
+    load_out.start()
+
+    barrier = pltpu.get_barrier_semaphore()
+    for peer in peers:
+        pl.semaphore_signal(barrier, inc=1, device_id=peer, device_id_type=pl.DeviceIdType.MESH)
+    lane = lax.broadcasted_iota(jnp.int32, (rows, LANES), 1)
+    gates = jnp.zeros((rows, LANES), F32)
+    for k in range(top):
+        gates += jnp.where(lane == ids_ref[:, k : k + 1], rw_ref[:, k : k + 1], 0.0)
+    gbuf[block(p * lines + z, rows), :] = gates
+    pl.semaphore_wait(barrier, len(peers))
+
+    t_in = start([copy(tok_ref, tbuf.at[block(z, rows), :], at_line(k)) for k in range(1, lines)])
+    w_in_ = start([copy(wd_ref, wbuf.at[block(p, wd_ref.shape[0]), :], at_plane(j)) for j in range(1, plane)])
+    g_slice = gbuf.at[block(p * lines + z, rows), :]
+    g_line = start([copy(g_slice, g_slice, at_line(k)) for k in range(1, lines)])
+    u_slice = ubuf.at[block(ep, rows), :]
+    u_plane = start([
+        copy(wup_ref.at[:, block(p ^ j, quarter)], u_slice, at_plane(j)) for j in range(1, plane)
+    ])
+    tbuf[block(z, rows), :] = tok_ref[...]
+    wbuf[block(p, wd_ref.shape[0]), :] = wd_ref[...]
+    ubuf[block(ep, rows), :] = wup_ref[:, block(p, quarter)]
+    got(g_line)
+    g_own = gbuf.at[block(p, group), :]
+    g_plane = start([copy(g_own, g_own, at_plane(j)) for j in range(1, plane)])
+    got(w_in_)
+    got(t_in)
+    part[...] = lax.dot_general(
+        tbuf[...], wbuf[...], (((1,), (1,)), ((), ())), preferred_element_type=F32
+    )
+    swap = start([copy(part.at[block(mate, half_rows), :], other, at_mate)])
+    got(swap)
+    own_rows = block(p * 2 + core, half_rows)
+    latent[own_rows, block(z, cols)] = (part[block(core, half_rows), :] + other[...]).astype(BF16)
+    l_slice = latent.at[own_rows, block(z, cols)]
+    l_line = start([copy(l_slice, l_slice, at_line(k)) for k in range(1, lines)])
+    got(l_line)
+    l_rows = latent.at[own_rows, :]
+    l_plane = start([copy(l_rows, l_rows, at_plane(j)) for j in range(1, plane)])
+    l_mate = start([copy(l_rows, l_rows, at_mate)])
+    got(u_plane)
+    u_own = ubuf.at[block(z, plane * rows), :]
+    u_line = start([copy(u_own, u_own, at_line(k)) for k in range(1, lines)])
+    got(g_plane)
+    load_in.wait()
+    load_out.wait()
+
+    expert = ep // 2
+    glane = lax.broadcasted_iota(jnp.int32, (group, LANES), 1)
+
+    y_core = []
+    for j in range(plane):
+        if j > 0:
+            got([l_plane[j - 1]])
+            mine = latent.at[block((p ^ j) * 2 + core, half_rows), :]
+            l_mate += start([copy(mine, mine, at_mate)])
+        got([l_mate[j]])
+        weight = jnp.sum(jnp.where(glane == expert, gbuf[block(p ^ j, group), :], 0.0), axis=1, keepdims=True)
+        pre = jnp.dot(latent[block(p ^ j, group), :], win[...], preferred_element_type=F32)
+        pre = jnp.maximum(pre, 0.0)
+        hidden = (pre * pre).astype(BF16)
+        ysend[j] = (
+            weight * jnp.dot(hidden, wout[:, block(mate, feat)], preferred_element_type=F32)
+        ).astype(BF16)
+        y_core += start([copy(ysend.at[j], ycore.at[j], at_mate)])
+        ykeep[j] = weight * jnp.dot(hidden, wout[:, block(core, feat)], preferred_element_type=F32)
+    y_plane = []
+    for j in range(1, plane):
+        got([y_core[j]])
+        xsend[j] = (ykeep[j] + ycore[j].astype(F32)).astype(BF16)
+        y_plane += start([copy(xsend.at[j], yrecv.at[j], at_plane(j))])
+    got([y_core[0]])
+    total = ykeep[0] + ycore[0].astype(F32)
+    for j in range(1, plane):
+        got([y_plane[j - 1]])
+        total += yrecv[j].astype(F32)
+    ykeep[0] = total
+    zsend[...] = total.astype(BF16)
+    z_line = start([
+        copy(zsend.at[block(z ^ k, rows), :], zrecv.at[k], at_line(k)) for k in range(1, lines)
+    ])
+    got(z_line)
+    mixed = ykeep[0, block(z, rows), :]
+    for k in range(1, lines):
+        mixed += zrecv[k].astype(F32)
+    mbuf[block(p, rows), block(core, feat)] = mixed.astype(BF16)
+    m_own = mbuf.at[block(p, rows), block(core, feat)]
+    m_plane = start([copy(m_own, m_own, at_plane(j)) for j in range(1, plane)])
+    m_mate = start([copy(m_own, m_own, at_mate)])
+    for j in range(1, plane):
+        got([m_plane[j - 1]])
+        m_slice = mbuf.at[block(p ^ j, rows), block(core, feat)]
+        m_mate += start([copy(m_slice, m_slice, at_mate)])
+    got(u_line)
+    got(m_mate)
+    obuf[...] = jnp.dot(mbuf[...], ubuf[...], preferred_element_type=F32).astype(BF16)
+    o_plane = start([
+        copy(obuf.at[block(p ^ j, rows), :], out_ref.at[:, block(p, quarter)], at_plane(j))
+        for j in range(1, plane)
+    ])
+    out_ref[:, block(p, quarter)] = obuf[block(p, rows), :]
+    got(o_plane)
+    for c in started:
+        c.wait_send()
+
+
+def fused(tokens, w_down, w_in, w_out, w_up, expert_ids, route_weights, lines, plane):
+    count, model = tokens.shape
+    width = w_in.shape[1]
+    hidden = w_in.shape[2]
+    group = count * lines
+    everyone = group * plane
+    feat = width // 2
+    quarter = w_up.shape[1] // plane
+    copies = 6 * (lines - 1) + 6 * (plane - 1) + 2 + (plane - 1) * 2 + plane * 2 + 8
+    vmem = pl.BlockSpec(memory_space=pltpu.VMEM)
+    hbm = pl.BlockSpec(memory_space=pl.ANY)
+    return pl.pallas_call(
+        functools.partial(fused_kernel, lines, plane),
+        out_shape=jax.ShapeDtypeStruct((count, w_up.shape[1]), BF16),
+        in_specs=[vmem, vmem, hbm, hbm, vmem, vmem, vmem],
+        out_specs=vmem,
+        scratch_shapes=[
+            pltpu.VMEM((group, model), BF16),
+            pltpu.VMEM((w_down.shape[1] * plane, model), BF16),
+            pltpu.VMEM((everyone, LANES), F32),
+            pltpu.VMEM((width, quarter), BF16),
+            pltpu.VMEM((group, w_down.shape[1] * plane), F32),
+            pltpu.VMEM((group // 2, w_down.shape[1] * plane), F32),
+            pltpu.VMEM((everyone, width), BF16),
+            pltpu.VMEM((width, hidden), BF16),
+            pltpu.VMEM((hidden, width), BF16),
+            pltpu.VMEM((plane, group, feat), F32),
+            pltpu.VMEM((plane, group, feat), BF16),
+            pltpu.VMEM((plane, group, feat), BF16),
+            pltpu.VMEM((plane, group, feat), BF16),
+            pltpu.VMEM((plane, group, feat), BF16),
+            pltpu.VMEM((group, feat), BF16),
+            pltpu.VMEM((lines, count, feat), BF16),
+            pltpu.VMEM((plane * count, width), BF16),
+            pltpu.VMEM((plane * count, quarter), BF16),
+            pltpu.SemaphoreType.DMA((copies,)),
+            pltpu.SemaphoreType.DMA((copies,)),
+            pltpu.SemaphoreType.DMA((2,)),
+        ],
+        compiler_params=pltpu.CompilerParams(
+            collective_id=0, has_side_effects=True, vmem_limit_bytes=60 * 2**20
+        ),
+    )(tokens, w_down.T, w_in[0], w_out[0], w_up, expert_ids, route_weights)
+
+
+def grid_of(devices):
+    bits = devices.bit_length() - 1
+    plane = 2 ** ((bits + 1) // 2)
+    return devices // plane, plane
+
+
 def solution(mesh):
     in_specs = (
         P(("groups", "ep"), "tp"),
@@ -82,6 +301,15 @@
         P(("groups", "ep"), None),
     )
     out_specs = P(("groups", "ep"), "tp")
-    return jax.shard_map(
-        per_device, mesh=mesh, in_specs=in_specs, out_specs=out_specs, check_vma=False
-    )
+    devices = mesh.shape["ep"]
+    lines, plane = grid_of(devices)
+
+    def body(tokens, w_down, w_in, w_out, w_up, expert_ids, route_weights):
+        args = (tokens, w_down, w_in, w_out, w_up, expert_ids, route_weights)
+        everyone = tokens.shape[0] * devices
+        resident = everyone * w_in.shape[1] * 10
+        if resident <= 2**24 and lines * plane == devices and mesh.shape["tp"] == 2:
+            return fused(*args, lines, plane)
+        return per_device(*args)
+
+    return jax.shard_map(body, mesh=mesh, in_specs=in_specs, out_specs=out_specs, check_vma=False)

time: 245 us -> 98.2 us (0.40)
  waiting for transfers between devices: 164 us -> 0 us
  Pallas kernels: 0 us -> 91 us
  starting transfers between devices: 30.2 us -> 0 us
  between operations: 13.6 us -> 0.01 us
  matrix products: 11.1 us -> 0 us
  blocking collectives: 8.33 us -> 0 us
  other arithmetic: 5.6 us -> 0 us
  local copies, waits for them, and re-layouts: 11.2 us -> 6.99 us
    pallas_call x0 -> x1, Pallas kernels: none -> 91 us  [fused(): pl.pallas_call(functools.partial(fused_kernel, lines, plane), out_shape=j...]
    all_gather x2 -> x0, waiting for transfers between devices: 77 us -> none  [the longest x1 77 us: per_device(): lax.all_gather(w_down, 'ep', axis=1, tiled=True)]
    all_to_all x2 -> x0, waiting for transfers between devices: 44.7 us -> none  [the longest x1 23.4 us: per_device(): lax.all_to_all(sending, 'ep', split_axis=0, concat_axis=0, tiled=True)]
    ppermute x2 -> x0, waiting for transfers between devices: 41.2 us -> none  [swapped(): return lax.ppermute(value, axis, pairs)]
    all_to_all x2 -> x0, starting transfers between devices: 27.2 us -> none  [the longest x1 23 us: per_device(): lax.all_to_all(sending, 'ep', split_axis=0, concat_axis=0, tiled=True)]
    dot_general x4 -> x0, matrix products: 11.1 us -> none  [the longest x1 3.74 us: per_device(): jnp.dot(mixed, lax.all_gather(w_up, 'ep', axis=0, tiled=True), preferred_...]
    psum x2 -> x0, blocking collectives: 8.33 us -> none  [the longest x1 4.17 us: per_device(): mixed = lax.psum(mixed_part, 'tp').astype(jnp.bfloat16)]
    unnamed x9 -> x4, local copies, waits for them, and re-layouts: 1.21 us -> 6.99 us
  transfers between devices with their start and end apart: 6 -> 0, of which waited for: 5 -> 0; matrix products, arithmetic and copies ran while one was open for 7% -> 0% of each run, Pallas kernels for 0% -> 0%
where the time goes in v1:
time: 98.2 us; the launch traced here: 98 us
  Pallas kernels  91 us (93%)
  local copies, waits for them, and re-layouts  6.99 us (7%)
    pallas_call x1, Pallas kernels, fused(): pl.pallas_call(functools.partial(fused_kernel, lines, plane), out_shape=j...  91 us
    unnamed x4, local copies, waits for them, and re-layouts  6.99 us

profile of v1, /device:TPU:0, one launch (start us, length us, event | category | flops | bytes accessed | tf_op | source)
XLA Modules:
  0.0 98.0 jit_solution(11143251897376959670)
XLA Ops:
  0.0 1.4 %copy.9.ids_ref = s32[64,3]{1,0:T(8,128)} copy(s32[64,3]{0,1:T(4,128)} %param.12) | data formatting | bytes 1536 | tf_op args[5]
  1.4 1.4 %copy.10.rw_ref = f32[64,3]{1,0:T(8,128)} copy(f32[64,3]{0,1:T(4,128)} %param.13) | data formatting | bytes 1536 | tf_op args[6]
  2.8 2.6 %copy.8 = bf16[1,1024,672]{2,1,0:T(8,128)(2,1)} copy(bf16[1,1024,672]{1,2,0:T(8,128)(2,1)} %param.9) | data formatting | bytes 2752512 | tf_op args[2]
  5.3 91.0 %shard_map.73 = bf16[64,2048]{1,0:T(8,128)(2,1)} custom-call(bf16[64,2048]{1,0:T(8,128)(2,1)} %tok_ref.1, bf16[64,2048]{1,0:T(8,128)(2,1)} %bitcast.5, bf16[1024,672]{1,0:T(8,128)(2,1)} %bitcast.3, bf16[672,1024]{1,0:T(8,128)(2,1)} %bitcast.4, bf16[64,2048]{1,0:T(8,128)(2,1)} %wup_ref.1, s32[64,3]{1,0:T(8,128)} %copy.9.ids_ref, f32[64,3]{1,0:T(8,128)} %copy.10.rw_ref), custom_call_target="tpu_custom_call" | custom-call | tf_op jit(solution)/shard_map/pallas_call | solution.py:253
  96.3 1.7 %copy.12 = bf16[64,2048]{1,0:T(8,128)(2,1)} copy(bf16[64,2048]{1,0:T(8,128)(2,1)} %shard_map.73) | data formatting | bytes 524288

commit v2 on v0

--- a/solution.py
+++ b/solution.py
@@ -1,7 +1,15 @@
 import jax
 import jax.numpy as jnp
 from jax import lax
+from jax.experimental import pallas as pl
+from jax.experimental.pallas import tpu as pltpu
 from jax.sharding import PartitionSpec as P
+
+F32 = jnp.float32
+BF16 = jnp.bfloat16
+LINKS = 2**4
+CHUNKS = 4
+COPIES = 128
 
 
 def swapped(value, axis, apart):
@@ -71,6 +79,254 @@
     return layer_out.astype(jnp.bfloat16)
 
 
+def fused_kernel(
+    tok_ref, wd_ref, win_hbm, wout_hbm, wup_ref, ids_ref, rw_ref, out_ref,
+    tbuf, wbuf, gbuf, ubuf, part, other, latent, win, wout, ykeep, ysend, ycore,
+    xsend, yrecv, zsend, zrecv, mbuf, obuf, send_sem, recv_sem, local_sem,
+):
+    ep = lax.axis_index("ep")
+    core = lax.axis_index("tp")
+    p = lax.rem(ep, 4)
+    z = ep // 4
+    x = lax.rem(ep, 2)
+    y = lax.rem(ep // 2, 2)
+    z0 = lax.rem(ep // 4, 2)
+    z1 = ep // 8
+    mate = 1 - core
+    top, rows = ids_ref.shape
+    model = tok_ref.shape[1]
+    group = 4 * rows
+    cols = wd_ref.shape[0]
+    feat = latent.shape[1] // 2
+    quarter = ubuf.shape[1]
+    experts = gbuf.shape[0] // LINKS
+    ids = iter(range(send_sem.shape[0]))
+
+    def at(mask):
+        return {"ep": ep ^ mask, "tp": core}
+
+    at_mate = {"ep": ep, "tp": mate}
+    peers = [at(mask) for mask in (1, 2, 3, 4, 8, 12)] + [at_mate]
+    started = []
+
+    def send(src, dst, device):
+        i = next(ids)
+        c = pltpu.make_async_remote_copy(
+            src_ref=src, dst_ref=dst, send_sem=send_sem.at[i], recv_sem=recv_sem.at[i],
+            device_id=device, device_id_type=pl.DeviceIdType.MESH,
+        )
+        c.start()
+        started.append(c)
+        return c
+
+    def got(*copies):
+        for c in copies:
+            c.wait_recv()
+
+    def block(index, size):
+        return pl.ds(pl.multiple_of(index * size, size), size)
+
+    barrier = pltpu.get_barrier_semaphore()
+    for peer in peers:
+        pl.semaphore_signal(barrier, inc=1, device_id=peer, device_id_type=pl.DeviceIdType.MESH)
+    pair = 2 * cols
+    loads = [pltpu.make_async_copy(wout_hbm, wout, local_sem.at[8])]
+    for n in range(8):
+        a, b, c = n // 4, n // 2 % 2, n % 2
+        loads.append(pltpu.make_async_copy(
+            win_hbm.at[:, pl.ds((a * 4 + b * 2 + c) * pair, pair)],
+            win.at[:, pl.ds((c * 4 + b * 2 + a) * pair, pair)],
+            local_sem.at[n],
+        ))
+    for load in loads:
+        load.start()
+    lane = lax.broadcasted_iota(jnp.int32, (experts, rows), 0)
+    gates = jnp.zeros((experts, rows), F32)
+    for k in range(top):
+        gates += jnp.where(lane == ids_ref[k : k + 1, :], rw_ref[k : k + 1, :], 0.0)
+    gbuf[block(p * 4 + z, experts), :] = gates
+    pl.semaphore_wait(barrier, len(peers))
+
+    step = model // CHUNKS
+    t_slot, w_slot = block(y * 2 + z0, rows), block(z1 * 2 + x, cols)
+    t_far, w_far = [], []
+    for n in range(CHUNKS):
+        part_n = pl.ds(n * step, step)
+        t_far.append(send(tok_ref.at[:, part_n], tbuf.at[t_slot, part_n], at(4)))
+        w_far.append(send(wd_ref.at[:, part_n], wbuf.at[w_slot, part_n], at(8)))
+    arrivals = [send(tok_ref, tbuf.at[t_slot, :], at(2)), send(wd_ref, wbuf.at[w_slot, :], at(1))]
+    tbuf[t_slot, :] = tok_ref[...]
+    wbuf[w_slot, :] = wd_ref[...]
+    ubuf[block(ep, rows), :] = wup_ref[:, block(p, quarter)]
+    g_slice = gbuf.at[block(p * 4 + z, experts), :]
+    g_line = [send(g_slice, g_slice, at(4 * k)) for k in (1, 2, 3)]
+    for n in range(CHUNKS):
+        part_n = pl.ds(n * step, step)
+        got(t_far[n])
+        t_next = tbuf.at[block(y * 2 + (1 - z0), rows), part_n]
+        arrivals.append(send(t_next, t_next, at(2)))
+        got(w_far[n])
+        w_next = wbuf.at[block((1 - z1) * 2 + x, cols), part_n]
+        arrivals.append(send(w_next, w_next, at(1)))
+    got(*g_line)
+    g_own = gbuf.at[block(p, 4 * experts), :]
+    g_plane = [send(g_own, g_own, at(j)) for j in (1, 2, 3)]
+    got(*arrivals)
+    part[...] = lax.dot_general(
+        tbuf[...], wbuf[...], (((1,), (1,)), ((), ())), preferred_element_type=F32
+    )
+    got(send(part.at[block(mate, 2 * rows), :], other, at_mate))
+
+    def piece(xx, zz1, yy, zz0):
+        return latent.at[block((core * 2 + xx) * 2 + zz1, 2 * rows), block(yy * 2 + zz0, 4 * cols)]
+
+    own = piece(x, z1, y, z0)
+    own[...] = (part[block(core, 2 * rows), :] + other[...]).astype(BF16)
+    l_line = {k: send(own, own, at(4 * k)) for k in (1, 2, 3)}
+    l_plane = {}
+    for k in range(4):
+        if k > 0:
+            got(l_line[k])
+        src = piece(x, z1 ^ (k // 2), y, z0 ^ (k % 2))
+        for j in (2, 1, 3):
+            l_plane[j, k] = send(src, src, at(j))
+    u_slice = ubuf.at[block(ep, rows), :]
+    u_plane = [send(wup_ref.at[:, block(p ^ j, quarter)], u_slice, at(j)) for j in (1, 2, 3)]
+
+    def to_mate(xx, columns):
+        src = latent.at[block(core * 2 + xx, group), columns]
+        return send(src, src, at_mate)
+
+    got(*[l_plane[2, k] for k in range(4)])
+    near = to_mate(x, pl.ds(0, 2 * feat))
+    got(*[l_plane[1, k] for k in range(4)])
+    far = [to_mate(1 - x, block(y, feat))]
+    got(*u_plane)
+    u_own = ubuf.at[block(z, 4 * rows), :]
+    u_line = [send(u_own, u_own, at(4 * k)) for k in (1, 2, 3)]
+    got(*g_plane)
+    for load in loads:
+        load.wait()
+    gate_rows = gbuf[...].T
+    glane = lax.broadcasted_iota(jnp.int32, gate_rows.shape, 1)
+    expert = ep // 2
+    y_core, y_plane = {}, {}
+
+    def compute(j):
+        gi = p ^ j
+        weight = jnp.concatenate([
+            jnp.sum(jnp.where(glane == (gi * 4 + k) * experts + expert, gate_rows, 0.0), axis=1, keepdims=True)
+            for k in range(4)
+        ], axis=0)
+        pre = lax.dot_general(
+            latent[block(gi, group), :], win[...], (((1,), (1,)), ((), ())), preferred_element_type=F32
+        )
+        pre = jnp.maximum(pre, 0.0)
+        hidden = (pre * pre).astype(BF16)
+        ysend[j] = (
+            weight * jnp.dot(hidden, wout[:, block(mate, feat)], preferred_element_type=F32)
+        ).astype(BF16)
+        y_core[j] = send(ysend.at[j], ycore.at[j], at_mate)
+        ykeep[j] = weight * jnp.dot(hidden, wout[:, block(core, feat)], preferred_element_type=F32)
+
+    def drain(j):
+        got(y_core[j])
+        xsend[j] = (ykeep[j] + ycore[j].astype(F32)).astype(BF16)
+        for k in (3, 2, 1, 0):
+            r = block(z ^ k, rows)
+            y_plane[j, k] = send(xsend.at[j, r, :], yrecv.at[j, r, :], at(j))
+
+    got(near)
+    compute(2)
+    compute(0)
+    drain(2)
+    got(*[l_plane[3, k] for k in range(4)])
+    far.append(to_mate(1 - x, block(1 - y, feat)))
+    got(*far)
+    compute(3)
+    compute(1)
+    drain(3)
+    drain(1)
+    got(y_core[0])
+    z_line = {}
+    for k in (3, 2, 1, 0):
+        r = block(z ^ k, rows)
+        total = ykeep[0, r, :] + ycore[0, r, :].astype(F32)
+        for j in (2, 3, 1):
+            got(y_plane[j, k])
+            total += yrecv[j, r, :].astype(F32)
+        if k > 0:
+            zsend[k] = total.astype(BF16)
+            z_line[k] = send(zsend.at[k], zrecv.at[k], at(4 * k))
+        else:
+            mixed = total
+    for k in (1, 2, 3):
+        got(z_line[k])
+        mixed += zrecv[k].astype(F32)
+    mbuf[block(p, rows), block(core, feat)] = mixed.astype(BF16)
+    m_own = mbuf.at[block(p, rows), block(core, feat)]
+    m_plane = [send(m_own, m_own, at(j)) for j in (1, 2, 3)]
+    m_mate = [send(m_own, m_own, at_mate)]
+    for j in (1, 2, 3):
+        got(m_plane[j - 1])
+        m_slice = mbuf.at[block(p ^ j, rows), block(core, feat)]
+        m_mate.append(send(m_slice, m_slice, at_mate))
+    got(*u_line)
+    got(*m_mate)
+    obuf[...] = jnp.dot(mbuf[...], ubuf[...], preferred_element_type=F32).astype(BF16)
+    o_plane = [
+        send(obuf.at[block(p ^ j, rows), :], out_ref.at[:, block(p, quarter)], at(j)) for j in (1, 2, 3)
+    ]
+    out_ref[:, block(p, quarter)] = obuf[block(p, rows), :]
+    got(*o_plane)
+    for c in started:
+        c.wait_send()
+
+
+def fused(tokens, w_down, w_in, w_out, w_up, expert_ids, route_weights):
+    count, model = tokens.shape
+    width = w_in.shape[1]
+    hidden = w_in.shape[2]
+    group = 4 * count
+    cols = 4 * w_down.shape[1]
+    feat = width // 2
+    quarter = w_up.shape[1] // 4
+    vmem = pl.BlockSpec(memory_space=pltpu.VMEM)
+    hbm = pl.BlockSpec(memory_space=pl.ANY)
+    return pl.pallas_call(
+        fused_kernel,
+        out_shape=jax.ShapeDtypeStruct((count, w_up.shape[1]), BF16),
+        in_specs=[vmem, vmem, hbm, hbm, vmem, vmem, vmem],
+        out_specs=vmem,
+        scratch_shapes=[
+            pltpu.VMEM((group, model), BF16),
+            pltpu.VMEM((cols, model), BF16),
+            pltpu.VMEM((LINKS * (LINKS // 2), count), F32),
+            pltpu.VMEM((width, quarter), BF16),
+            pltpu.VMEM((group, cols), F32),
+            pltpu.VMEM((group // 2, cols), F32),
+            pltpu.VMEM((LINKS * count, width), BF16),
+            pltpu.VMEM((hidden, width), BF16),
+            pltpu.VMEM((hidden, width), BF16),
+            pltpu.VMEM((4, group, feat), F32),
+            pltpu.VMEM((4, group, feat), BF16),
+            pltpu.VMEM((4, group, feat), BF16),
+            pltpu.VMEM((4, group, feat), BF16),
+            pltpu.VMEM((4, group, feat), BF16),
+            pltpu.VMEM((4, count, feat), BF16),
+            pltpu.VMEM((4, count, feat), BF16),
+            pltpu.VMEM((group, width), BF16),
+            pltpu.VMEM((group, quarter), BF16),
+            pltpu.SemaphoreType.DMA((COPIES,)),
+            pltpu.SemaphoreType.DMA((COPIES,)),
+            pltpu.SemaphoreType.DMA((9,)),
+        ],
+        compiler_params=pltpu.CompilerParams(
+            collective_id=0, has_side_effects=True, vmem_limit_bytes=60 * 2**20
+        ),
+    )(tokens, w_down.T, w_in[0].T, w_out[0], w_up, expert_ids.T, route_weights.T)
+
+
 def solution(mesh):
     in_specs = (
         P(("groups", "ep"), "tp"),
@@ -82,6 +338,14 @@
         P(("groups", "ep"), None),
     )
     out_specs = P(("groups", "ep"), "tp")
-    return jax.shard_map(
-        per_device, mesh=mesh, in_specs=in_specs, out_specs=out_specs, check_vma=False
-    )
+    devices = mesh.shape["ep"]
+
+    def body(tokens, w_down, w_in, w_out, w_up, expert_ids, route_weights):
+        args = (tokens, w_down, w_in, w_out, w_up, expert_ids, route_weights)
+        everyone = tokens.shape[0] * devices
+        resident = everyone * w_in.shape[1] * 10
+        if resident <= 2**24 and devices == LINKS and mesh.shape["tp"] == 2:
+            return fused(*args)
+        return per_device(*args)
+
+    return jax.shard_map(body, mesh=mesh, in_specs=in_specs, out_specs=out_specs, check_vma=False)

time: 245 us -> 86.9 us (0.35)
  waiting for transfers between devices: 164 us -> 0 us
  Pallas kernels: 0 us -> 85 us
  starting transfers between devices: 30.2 us -> 0 us
  between operations: 13.6 us -> 0.01 us
  matrix products: 11.1 us -> 0 us
  local copies, waits for them, and re-layouts: 11.2 us -> 1.67 us
  blocking collectives: 8.33 us -> 0 us
  other arithmetic: 5.6 us -> 0 us
    pallas_call x0 -> x1, Pallas kernels: none -> 85 us  [fused(): pl.pallas_call(fused_kernel, out_shape=jax.ShapeDtypeStruct((count, w_up....]
    all_gather x2 -> x0, waiting for transfers between devices: 77 us -> none  [the longest x1 77 us: per_device(): lax.all_gather(w_down, 'ep', axis=1, tiled=True)]
    all_to_all x2 -> x0, waiting for transfers between devices: 44.7 us -> none  [the longest x1 23.4 us: per_device(): lax.all_to_all(sending, 'ep', split_axis=0, concat_axis=0, tiled=True)]
    ppermute x2 -> x0, waiting for transfers between devices: 41.2 us -> none  [swapped(): return lax.ppermute(value, axis, pairs)]
    all_to_all x2 -> x0, starting transfers between devices: 27.2 us -> none  [the longest x1 23 us: per_device(): lax.all_to_all(sending, 'ep', split_axis=0, concat_axis=0, tiled=True)]
    dot_general x4 -> x0, matrix products: 11.1 us -> none  [the longest x1 3.74 us: per_device(): jnp.dot(mixed, lax.all_gather(w_up, 'ep', axis=0, tiled=True), preferred_...]
    psum x2 -> x0, blocking collectives: 8.33 us -> none  [the longest x1 4.17 us: per_device(): mixed = lax.psum(mixed_part, 'tp').astype(jnp.bfloat16)]
    gather x3 -> x0, local copies, waits for them, and re-layouts: 5.34 us -> none  [the longest x2 3.27 us: per_device(): picked = summed[place] * route_weights.reshape(count * top)[:, None]]
  transfers between devices with their start and end apart: 6 -> 0, of which waited for: 5 -> 0; matrix products, arithmetic and copies ran while one was open for 7% -> 0% of each run, Pallas kernels for 0% -> 0%
where the time goes in v2:
time: 86.9 us; the launch traced here: 86.7 us
  Pallas kernels  85 us (98%)
  local copies, waits for them, and re-layouts  1.67 us (2%)
    pallas_call x1, Pallas kernels, fused(): pl.pallas_call(fused_kernel, out_shape=jax.ShapeDtypeStruct((count, w_up....  85 us

profile of v2, /device:TPU:0, one launch (start us, length us, event | category | flops | bytes accessed | tf_op | source)
XLA Modules:
  0.0 86.7 jit_solution(16139927981502841510)
XLA Ops:
  0.0 85.0 %shard_map.73 = bf16[64,2048]{1,0:T(8,128)(2,1)} custom-call(bf16[64,2048]{1,0:T(8,128)(2,1)} %tok_ref.1, bf16[64,2048]{1,0:T(8,128)(2,1)} %bitcast.9, bf16[672,1024]{1,0:T(8,128)(2,1)} %bitcast.7, bf16[672,1024]{1,0:T(8,128)(2,1)} %bitcast.8, bf16[64,2048]{1,0:T(8,128)(2,1)} %wup_ref.1, s32[3,64]{1,0:T(4,128)} %bitcast.10, f32[3,64]{1,0:T(4,128)} %bitcast.11), custom_call_target="tpu_custom_call" | custom-call | tf_op jit(solution)/shard_map/pallas_call | solution.py:296
  85.0 1.7 %copy.9 = bf16[64,2048]{1,0:T(8,128)(2,1)} copy(bf16[64,2048]{1,0:T(8,128)(2,1)} %shard_map.73) | data formatting | bytes 524288

commit v3 on v2

--- a/solution.py
+++ b/solution.py
@@ -171,6 +171,8 @@
     got(*g_line)
     g_own = gbuf.at[block(p, 4 * experts), :]
     g_plane = [send(g_own, g_own, at(j)) for j in (1, 2, 3)]
+    u_slice = ubuf.at[block(ep, rows), :]
+    u_plane = [send(wup_ref.at[:, block(p ^ j, quarter)], u_slice, at(j)) for j in (1, 2, 3)]
     got(*arrivals)
     part[...] = lax.dot_general(
         tbuf[...], wbuf[...], (((1,), (1,)), ((), ())), preferred_element_type=F32
@@ -183,27 +185,28 @@
     own = piece(x, z1, y, z0)
     own[...] = (part[block(core, 2 * rows), :] + other[...]).astype(BF16)
     l_line = {k: send(own, own, at(4 * k)) for k in (1, 2, 3)}
-    l_plane = {}
+    got(*u_plane)
+    u_own = ubuf.at[block(z, 4 * rows), :]
+    u_line = [send(u_own, u_own, at(4 * k)) for k in (1, 2, 3)]
+    side, ahead = 1 + core, 2 - core
+    l_side, l_ahead, l_diag = [], [], []
     for k in range(4):
         if k > 0:
             got(l_line[k])
         src = piece(x, z1 ^ (k // 2), y, z0 ^ (k % 2))
-        for j in (2, 1, 3):
-            l_plane[j, k] = send(src, src, at(j))
-    u_slice = ubuf.at[block(ep, rows), :]
-    u_plane = [send(wup_ref.at[:, block(p ^ j, quarter)], u_slice, at(j)) for j in (1, 2, 3)]
-
+        l_side.append(send(src, src, at(side)))
+        l_ahead.append(send(src, src, at(ahead)))
+    for k in range(4):
+        got(l_side[k])
+        src = piece(x ^ (1 - core), z1 ^ (k // 2), y ^ core, z0 ^ (k % 2))
+        l_diag.append(send(src, src, at(ahead)))
     def to_mate(xx, columns):
         src = latent.at[block(core * 2 + xx, group), columns]
         return send(src, src, at_mate)
 
-    got(*[l_plane[2, k] for k in range(4)])
+    got(*l_ahead)
     near = to_mate(x, pl.ds(0, 2 * feat))
-    got(*[l_plane[1, k] for k in range(4)])
     far = [to_mate(1 - x, block(y, feat))]
-    got(*u_plane)
-    u_own = ubuf.at[block(z, 4 * rows), :]
-    u_line = [send(u_own, u_own, at(4 * k)) for k in (1, 2, 3)]
     got(*g_plane)
     for load in loads:
         load.wait()
@@ -240,7 +243,7 @@
     compute(2)
     compute(0)
     drain(2)
-    got(*[l_plane[3, k] for k in range(4)])
+    got(*l_diag)
     far.append(to_mate(1 - x, block(1 - y, feat)))
     got(*far)
     compute(3)

time: 86.9 us -> 77.1 us (0.89)
  Pallas kernels: 85 us -> 75.3 us
    pallas_call x1, Pallas kernels: 85 us -> 75.3 us  [fused(): pl.pallas_call(fused_kernel, out_shape=jax.ShapeDtypeStruct((count, w_up....]
where the time goes in v3:
time: 77.1 us; the launch traced here: 76.9 us
  Pallas kernels  75.3 us (98%)
  local copies, waits for them, and re-layouts  1.67 us (2%)
    pallas_call x1, Pallas kernels, fused(): pl.pallas_call(fused_kernel, out_shape=jax.ShapeDtypeStruct((count, w_up....  75.3 us
    unnamed x1, local copies, waits for them, and re-layouts  1.67 us

profile of v3, /device:TPU:0, one launch (start us, length us, event | category | flops | bytes accessed | tf_op | source)
XLA Modules:
  0.0 76.9 jit_solution(8838333265149131063)
XLA Ops:
  0.0 75.3 %shard_map.73 = bf16[64,2048]{1,0:T(8,128)(2,1)} custom-call(bf16[64,2048]{1,0:T(8,128)(2,1)} %tok_ref.1, bf16[64,2048]{1,0:T(8,128)(2,1)} %bitcast.9, bf16[672,1024]{1,0:T(8,128)(2,1)} %bitcast.7, bf16[672,1024]{1,0:T(8,128)(2,1)} %bitcast.8, bf16[64,2048]{1,0:T(8,128)(2,1)} %wup_ref.1, s32[3,64]{1,0:T(4,128)} %bitcast.10, f32[3,64]{1,0:T(4,128)} %bitcast.11), custom_call_target="tpu_custom_call" | custom-call | tf_op jit(solution)/shard_map/pallas_call | solution.py:299
  75.3 1.7 %copy.9 = bf16[64,2048]{1,0:T(8,128)(2,1)} copy(bf16[64,2048]{1,0:T(8,128)(2,1)} %shard_map.73) | data formatting | bytes 524288

commit v4 on v3

--- a/solution.py
+++ b/solution.py
@@ -8,7 +8,7 @@
 F32 = jnp.float32
 BF16 = jnp.bfloat16
 LINKS = 2**4
-CHUNKS = 4
+CHUNKS = 8
 COPIES = 128
 
 
@@ -239,23 +239,22 @@
             r = block(z ^ k, rows)
             y_plane[j, k] = send(xsend.at[j, r, :], yrecv.at[j, r, :], at(j))
 
-    got(near)
-    compute(2)
-    compute(0)
-    drain(2)
     got(*l_diag)
     far.append(to_mate(1 - x, block(1 - y, feat)))
-    got(*far)
+    got(near, *far)
     compute(3)
     compute(1)
     drain(3)
+    compute(2)
     drain(1)
+    compute(0)
+    drain(2)
     got(y_core[0])
     z_line = {}
     for k in (3, 2, 1, 0):
         r = block(z ^ k, rows)
         total = ykeep[0, r, :] + ycore[0, r, :].astype(F32)
-        for j in (2, 3, 1):
+        for j in (3, 1, 2):
             got(y_plane[j, k])
             total += yrecv[j, r, :].astype(F32)
         if k > 0:

time: 77.1 us -> 77 us (level)
  no operation moved by 1% of the time
where the time goes in v4:
time: 77 us; the launch traced here: 76.8 us
  Pallas kernels  75.1 us (98%)
  local copies, waits for them, and re-layouts  1.67 us (2%)
    pallas_call x1, Pallas kernels, fused(): pl.pallas_call(fused_kernel, out_shape=jax.ShapeDtypeStruct((count, w_up....  75.1 us
    unnamed x1, local copies, waits for them, and re-layouts  1.67 us

profile of v4, /device:TPU:0, one launch (start us, length us, event | category | flops | bytes accessed | tf_op | source)
XLA Modules:
  0.0 76.8 jit_solution(4651805711486263034)
XLA Ops:
  0.0 75.1 %shard_map.73 = bf16[64,2048]{1,0:T(8,128)(2,1)} custom-call(bf16[64,2048]{1,0:T(8,128)(2,1)} %tok_ref.1, bf16[64,2048]{1,0:T(8,128)(2,1)} %bitcast.9, bf16[672,1024]{1,0:T(8,128)(2,1)} %bitcast.7, bf16[672,1024]{1,0:T(8,128)(2,1)} %bitcast.8, bf16[64,2048]{1,0:T(8,128)(2,1)} %wup_ref.1, s32[3,64]{1,0:T(4,128)} %bitcast.10, f32[3,64]{1,0:T(4,128)} %bitcast.11), custom_call_target="tpu_custom_call" | custom-call | tf_op jit(solution)/shard_map/pallas_call | solution.py:298
  75.1 1.7 %copy.9 = bf16[64,2048]{1,0:T(8,128)(2,1)} copy(bf16[64,2048]{1,0:T(8,128)(2,1)} %shard_map.73) | data formatting | bytes 524288
